TPU v7x, 32 devices: a whole 2x2x4 slice. The times are simulated.
32 devices in a mesh: gx: 4 (over y, x), gy: 2 (over core), gz: 4 (over z).
Axes of the slice: x: 2, y: 2, z: 4, core: 2. Of those that a mesh axis runs over, the one named last changes fastest.
Arguments:
- patches: bfloat16 [512, 6144], P(('gz', 'gx'), 'gy'), may hold values from -6 to 6
- modality: int32 [512], P(('gz', 'gx')), may hold values from 0 to 2
- gains: float32 [3, 6144], P(None, 'gy'), may hold values from 0.1 to 1.9
- biases: float32 [3, 6144], P(None, 'gy'), may hold values from -3 to 3
- weights: bfloat16 [3, 6144, 3072], P(None, ('gy', 'gz'), 'gx'), may hold values from -0.078125 to 0.078125
- segments: int32 [4, 128], P('gz'), may hold values from 0 to 3, never falling along the last dimension, each value on 1 to 64 neighbouring positions
- cotangent: bfloat16 [512, 3072], P(('gz', 'gy'), 'gx'), may hold values from -6 to 6
Outputs:
- attended: bfloat16 [512, 3072], P(('gz', 'gy'), 'gx')
- patch_gradient: float32 [512, 6144], P(('gz', 'gx'), 'gy')
Inputs may be any that keep to these rules, and one draw needn't show every extreme that they name: `segments`: within each pack the segment ids never fall, and each segment holds at most half of 128 patches.
All inputs are finite; a program needn't handle non-finite values.
Results may differ from a plain program's by a relative error of at most 0.02.
Values may be sent and summed in bfloat16 or wider, within the bound.
A program may use at most 64 MiB of HBM per device.

v0:
```python
import jax
import jax.numpy as jnp
from jax import lax
from jax.sharding import PartitionSpec as P

MODEL_WIDTH = 6144
HEAD_DIM = 128


EPS = 1e-06


def sum_over_width(totals):
    return lax.psum((totals[0], totals[1]), "gy")


def split_sum(partial_value):
    return lax.psum(partial_value, "gy").astype(jnp.float32)


def on_device(patches, modality, gains, biases, weights, segments, cotangent):
    values_f = patches.astype(jnp.float32)
    totals, squares = sum_over_width((jnp.sum(values_f, -1), jnp.sum(values_f * values_f, -1)))
    average = totals / MODEL_WIDTH
    variance = squares / MODEL_WIDTH - average * average
    mean_removed = values_f - average[:, None]
    inverse_deviation = lax.rsqrt(variance + EPS)[:, None]
    standardized_input = mean_removed * inverse_deviation
    levels = jnp.arange(gains.shape[0], dtype=jnp.int32)
    chosen = (modality[:, None] == levels[None, :])[:, :, None]
    gain_per_row = jnp.sum(jnp.where(chosen, gains[None], 0.0), 1)
    bias_per_row = jnp.sum(jnp.where(chosen, biases[None], 0.0), 1)
    layer_normalized = (standardized_input * gain_per_row + bias_per_row).astype(jnp.bfloat16)
    full_weights = lax.all_gather(weights, "gz", axis=1, tiled=True)
    partial_value = jnp.einsum(
        "rd,kdc->rkc",
        lax.all_gather(layer_normalized, "gx", axis=0, tiled=True),
        full_weights,
        preferred_element_type=jnp.float32,
    ).astype(jnp.bfloat16)
    pack_rows = partial_value.shape[0]
    own_rows = pack_rows // lax.axis_size("gy")
    offset = lax.axis_index("gy") * own_rows
    projected = split_sum(partial_value).astype(jnp.bfloat16)
    queries = lax.dynamic_slice_in_dim(projected[:, 0], offset, own_rows, 0)
    keys, values = (projected[:, 1], projected[:, 2])
    columns = full_weights.shape[2]
    head_count = columns // HEAD_DIM
    queries = queries.reshape(own_rows, head_count, HEAD_DIM)
    keys = keys.reshape(pack_rows, head_count, HEAD_DIM)
    values = values.reshape(pack_rows, head_count, HEAD_DIM)
    segment = segments[0]
    segment_query = lax.dynamic_slice_in_dim(segment, offset, own_rows, 0)
    allowed = (segment_query[:, None] == segment[None, :])[None]
    scaling = HEAD_DIM ** (-0.5)
    scores = jnp.einsum("qhd,khd->hqk", queries, keys, preferred_element_type=jnp.float32) * scaling
    exponent = jnp.where(allowed, jnp.exp(scores), 0.0)
    probs = exponent / jnp.sum(exponent, -1, keepdims=True)
    probs_b = probs.astype(jnp.bfloat16)
    attended = (
        jnp.einsum("hqk,khd->qhd", probs_b, values, preferred_element_type=jnp.float32)
        .astype(jnp.bfloat16)
        .reshape(own_rows, columns)
    )
    upstream = cotangent.reshape(own_rows, head_count, HEAD_DIM)
    dprobs = jnp.einsum("qhd,khd->hqk", upstream, values, preferred_element_type=jnp.float32)
    dvalues = jnp.einsum("hqk,qhd->khd", probs_b, upstream, preferred_element_type=jnp.float32)
    dscores = (probs * (dprobs - jnp.sum(probs * dprobs, -1, keepdims=True)) * scaling).astype(
        jnp.bfloat16
    )
    dqueries = jnp.einsum("hqk,khd->qhd", dscores, keys, preferred_element_type=jnp.float32)
    dkeys = jnp.einsum("hqk,qhd->khd", dscores, queries, preferred_element_type=jnp.float32)
    query_block = lax.dynamic_update_slice_in_dim(
        jnp.zeros((pack_rows, head_count, HEAD_DIM), jnp.float32), dqueries, offset, 0
    )
    stacked = (
        jnp.stack([query_block, dkeys, dvalues], 1)
        .reshape(pack_rows, 3, columns)
        .astype(jnp.bfloat16)
    )
    grad_proj = split_sum(stacked).astype(jnp.bfloat16)
    dnormed = lax.psum_scatter(
        jnp.einsum("rkc,kdc->rd", grad_proj, full_weights, preferred_element_type=jnp.float32),
        "gx",
        scatter_dimension=0,
        tiled=True,
    )
    normalized_gradient = dnormed * gain_per_row
    gradient_row_sum, weighted_row_sum = sum_over_width(
        (jnp.sum(normalized_gradient, -1), jnp.sum(normalized_gradient * standardized_input, -1))
    )
    patch_gradient = inverse_deviation * (
        normalized_gradient
        - gradient_row_sum[:, None] / MODEL_WIDTH
        - standardized_input * (weighted_row_sum[:, None] / MODEL_WIDTH)
    )
    return (attended, patch_gradient)


def solution(mesh):
    return jax.shard_map(
        on_device,
        mesh=mesh,
        in_specs=(
            P(("gz", "gx"), "gy"),
            P(("gz", "gx")),
            P(None, "gy"),
            P(None, "gy"),
            P(None, ("gy", "gz"), "gx"),
            P("gz", None),
            P(("gz", "gy"), "gx"),
        ),
        out_specs=(P(("gz", "gy"), "gx"), P(("gz", "gx"), "gy")),
        check_vma=False,
    )
```

profile of v0, /device:TPU:1, one launch (start us, length us, event | category | flops | bytes accessed | tf_op | source)
XLA Modules:
  0.0 362.5 jit_solution(14495759897900691260)
XLA Ops:
  7.2 0.0 copy-start
  7.2 0.0 copy-start.1
  7.2 0.0 copy-start.5
  7.2 0.0 copy-start.3
  7.2 0.0 copy-start.2
  7.2 0.0 all-gather.2.cloned.1.call-start
  7.3 0.7 all-gather.2.cloned.1.call-update
  8.0 0.0 all-reduce.5.cloned.1.call-start
  8.0 0.1 copy-done.1
  8.1 0.2 convert_reduce_fusion
  8.3 2.5 all-reduce.1
  10.8 0.0 copy-done.5
  10.8 0.0 copy-done.3
  10.8 0.0 copy-done.2
  10.8 0.2 select_reduce_fusion.1
  11.1 0.1 fusion.14
  11.2 11.8 %all_gather.6 = bf16[128,3072]{1,0:T(8,128)(2,1)S(1)} all-gather(bf16[32,3072]{1,0:T(8,128)(2,1)S(1)} %fusion.14), channel_id=1, replica_groups=mesh['gx'=4,'gy'=2,'gz'=4] {'gx'}, dimensions={0}, use_global_device_ids=true | all-gather | bytes 983040 | tf_op jit(solution)/shard_map/all_gather | solution.py:37
  23.0 0.0 copy-start.4
  23.0 232.8 %all-gather.2.cloned.1.call-done = bf16[3,3072,768]{2,1,0:T(8,128)(2,1)} async-done(((bf16[3,768,768]{2,1,0:T(8,128)(2,1)}), bf16[3,3072,768]{2,1,0:T(8,128)(2,1)}) %all-gather.2.cloned.1.call-update) | async-done | bytes 14155792 | tf_op jit(solution)/shard_map/all_gather | solution.py:34
  255.8 7.9 %convolution_convert_fusion = bf16[128,3,768]{2,0,1:T(8,128)(2,1)} fusion(bf16[3,3072,768]{2,1,0:T(8,128)(2,1)} %all-gather.2.cloned.1.call-done, bf16[128,3072]{1,0:T(8,128)(2,1)S(1)} %all_gather.6), kind=kOutput, calls=%fused_computation.2 | convolution fusion | flops 1812234240 | bytes 15532032 | tf_op jit(solution)/shard_map/rd,kdc->rkc/dot_general | solution.py:35
  263.6 0.0 all-reduce.5.cloned.1.call-update
  263.7 0.0 all-reduce.7.cloned.1.call-start
  263.7 0.0 copy-done.4
  263.7 0.1 dynamic-slice_bitcast_fusion
  263.8 0.1 broadcast_compare_fusion
  263.9 17.1 %all-reduce.5.cloned.1.call-done = bf16[128,3,768]{2,0,1:T(8,128)(2,1)} async-done(((bf16[128,3,768]{2,0,1:T(8,128)(2,1)}), bf16[128,3,768]{2,0,1:T(8,128)(2,1)}) %all-reduce.5.cloned.1.call-update) | async-done | bytes 589840 | tf_op jit(solution)/shard_map/psum | solution.py:18
  280.9 1.2 fusion.40
  282.1 0.1 reshape.89
  282.3 0.2 copy.34
  282.4 0.2 copy.33
  282.6 0.3 fusion.26
  282.9 0.0 copy-done
  282.9 0.3 convolution_convert_fusion.1
  283.2 0.2 convolution_bitcast_fusion.1
  283.3 0.3 convolution_bitcast_fusion.2
  283.6 0.3 convolution_convert_fusion.2
  284.0 0.1 copy.47
  284.1 0.1 copy.46
  284.3 0.2 copy.42
  284.5 2.5 dynamic_update_slice.4
  287.0 0.1 copy.45
  287.1 0.9 pad_maximum_fusion
  288.0 0.0 all-reduce.7.cloned.1.call-update
  288.0 0.0 reduce-scatter.2.cloned.1.call-start
  288.1 19.9 %all-reduce.7.cloned.1.call-done = bf16[128,3,768]{2,0,1:T(8,128)(2,1)} async-done(((bf16[128,3,768]{2,0,1:T(8,128)(2,1)}), bf16[128,3,768]{2,0,1:T(8,128)(2,1)}) %all-reduce.7.cloned.1.call-update) | async-done | bytes 589840 | tf_op jit(solution)/shard_map/psum | solution.py:18
  308.0 10.9 %convolution_bitcast_fusion = f32[128,3072]{1,0:T(8,128)} fusion(bf16[128,3,768]{2,0,1:T(8,128)(2,1)} %all-reduce.7.cloned.1.call-done, bf16[3,3072,768]{2,1,0:T(8,128)(2,1)} %all-gather.2.cloned.1.call-done), kind=kOutput, calls=%fused_computation.1 | convolution fusion | flops 1811939328 | bytes 16318464 | tf_op jit(solution)/shard_map/rkc,kdc->rd/dot_general | solution.py:83
  318.9 0.0 reduce-scatter.2.cloned.1.call-update
  318.9 0.2 fusion.7
  319.1 0.7 copy.69
  319.8 31.0 %reduce-scatter.2.cloned.1.call-done = f32[32,3072]{1,0:T(8,128)} async-done(((f32[128,3072]{1,0:T(8,128)}), f32[32,3072]{1,0:T(8,128)}) %reduce-scatter.2.cloned.1.call-update) | async-done | bytes 393232 | tf_op jit(solution)/shard_map/reduce_scatter | solution.py:82
  350.9 1.2 fusion.39
  352.1 2.9 all-reduce
  355.1 0.9 fusion.17
  (5 shorter events, 0.1 us)
Async XLA Ops:
  7.2 275.7 %copy-start = (bf16[64,768]{1,0:T(8,128)(2,1)S(1)}, bf16[64,768]{1,0:T(8,128)(2,1)}, u32[]{:S(2)}) copy-start(bf16[64,768]{1,0:T(8,128)(2,1)} %param.13) | copy-start | bytes 294916
  7.2 1.0 copy-start.1
  7.2 3.6 copy-start.5
  7.2 3.6 copy-start.3
  7.2 3.6 copy-start.2
  7.2 248.5 %all-gather.2.cloned.1.call-start = ((), (), s32[]{:S(2)}) async-start(), calls=%async_computation.1 | async-start | bytes 17694720 | tf_op jit(solution)/shard_map/all_gather | solution.py:34
  8.0 273.0 %all-reduce.5.cloned.1.call-start = ((), (), s32[]{:S(2)}) async-start(), calls=%async_computation.2 | async-start | bytes 1179648 | tf_op jit(solution)/shard_map/psum | solution.py:18
  23.0 240.7 %copy-start.4 = (s32[1,128]{1,0:T(1,128)S(1)}, s32[1,128]{1,0:T(1,128)}, u32[]{:S(2)}) copy-start(s32[1,128]{1,0:T(1,128)} %param.12) | copy-start | bytes 1540
  263.7 44.3 %all-reduce.7.cloned.1.call-start = ((), (), s32[]{:S(2)}) async-start(), calls=%async_computation.3 | async-start | bytes 1179648 | tf_op jit(solution)/shard_map/psum | solution.py:18
  288.0 62.8 %reduce-scatter.2.cloned.1.call-start = ((), (), s32[]{:S(2)}) async-start(), calls=%async_computation.4 | async-start | bytes 1966080 | tf_op jit(solution)/shard_map/reduce_scatter | solution.py:82
Sparse Core Ops, SparseCore 0:
  9.6 246.1 all-gather.1
  263.8 17.1 all-reduce.4
  288.2 19.7 all-reduce.6
  319.1 31.7 reduce-scatter.1
where the time goes:
time: 363 us; the launch traced here: 362 us
  waiting for transfers between devices  302 us (83%)
  matrix products  20.3 us (6%)
  blocking collectives  17.2 us (5%)
  between operations  14 us (4%)
  local copies, waits for them, and re-layouts  5.68 us (2%)
  other arithmetic  3.65 us (1%)
    all_gather x1, waiting for transfers between devices, on_device(): full_weights = lax.all_gather(weights, 'gz', axis=1, tiled=True)  233 us
    psum x2, waiting for transfers between devices, split_sum(): return lax.psum(partial_value, 'gy').astype(jnp.float32)  37 us
    reduce_scatter x1, waiting for transfers between devices, on_device(): lax.psum_scatter(jnp.einsum('rkc,kdc->rd', grad_proj, full_weights, prefe...  31 us
    all_gather x1, blocking collectives, on_device(): lax.all_gather(layer_normalized, 'gx', axis=0, tiled=True)  11.8 us
    dot_general x1, matrix products, on_device(): jnp.einsum('rkc,kdc->rd', grad_proj, full_weights, preferred_element_type...  10.9 us
    dot_general x1, matrix products, on_device(): jnp.einsum('rd,kdc->rkc', lax.all_gather(layer_normalized, 'gx', axis=0,...  7.86 us
  transfers between devices with their start and end apart: 4, of which 4 were waited for; matrix products, arithmetic and copies ran while one was open for 0% of the time, Pallas kernels for 0%

commit v1 on v0

--- a/solution.py
+++ b/solution.py
@@ -97,9 +97,72 @@
     return (attended, patch_gradient)
 
 
+def stationary(patches, modality, gains, biases, weights, segments, cotangent):
+    packs, parts, groups = lax.axis_size("gz"), lax.axis_size("gy"), lax.axis_size("gx")
+    values_f = patches.astype(jnp.float32)
+    rows, width = values_f.shape
+    mine = jnp.mean(values_f, -1)
+    spread = jnp.sum((values_f - mine[:, None]) ** 2, -1)
+    both = lax.all_gather(jnp.stack([mine, spread]), "gy")
+    average = jnp.mean(both[:, 0], 0)
+    variance = (jnp.sum(both[:, 1], 0) + width * jnp.sum((both[:, 0] - average) ** 2, 0)) / MODEL_WIDTH
+    inverse = lax.rsqrt(variance + EPS)[:, None]
+    xhat = (values_f - average[:, None]) * inverse
+    levels = jnp.arange(gains.shape[0], dtype=jnp.int32)
+    chosen = (modality[:, None] == levels[None, :])[:, :, None]
+    gain = jnp.sum(jnp.where(chosen, gains[None], 0.0), 1)
+    bias = jnp.sum(jnp.where(chosen, biases[None], 0.0), 1)
+    normed = (xhat * gain + bias).astype(jnp.bfloat16)
+    block, columns = weights.shape[1:]
+    share = columns // parts
+    heads = share // HEAD_DIM
+    moved = lax.all_to_all(normed.reshape(rows, packs, block), "gz", 1, 0, tiled=True)
+    moved = moved.reshape(packs, rows, block)
+    moved = lax.all_gather(moved, "gx", axis=1, tiled=True)
+    length = rows * groups
+    partial_value = jnp.einsum("prd,kdc->prkc", moved, weights, preferred_element_type=jnp.float32)
+    partial_value = partial_value.astype(jnp.bfloat16).reshape(packs, length, 3, parts, share)
+    partial_value = partial_value.transpose(0, 3, 1, 2, 4).reshape(packs * parts * length, 3 * share)
+    projected = lax.psum_scatter(partial_value, ("gz", "gy"), scatter_dimension=0, tiled=True)
+    projected = projected.reshape(length, 3, heads, HEAD_DIM)
+    queries, keys, values = projected[:, 0], projected[:, 1], projected[:, 2]
+    up = lax.all_to_all(cotangent, "gy", 1, 0, tiled=True).reshape(length, heads, HEAD_DIM)
+    segment = segments[0]
+    allowed = (segment[:, None] == segment[None, :])[None]
+    scaling = HEAD_DIM ** (-0.5)
+    f32 = dict(preferred_element_type=jnp.float32)
+    scores = jnp.einsum("qhd,khd->hqk", queries, keys, **f32) * scaling
+    exponent = jnp.where(allowed, jnp.exp(scores), 0.0)
+    probs = exponent / jnp.sum(exponent, -1, keepdims=True)
+    probs_b = probs.astype(jnp.bfloat16)
+    attended = jnp.einsum("hqk,khd->qhd", probs_b, values, **f32).astype(jnp.bfloat16)
+    attended = lax.all_to_all(attended.reshape(length, share), "gy", 0, 1, tiled=True)
+    dprobs = jnp.einsum("qhd,khd->hqk", up, values, **f32)
+    dvalues = jnp.einsum("hqk,qhd->khd", probs_b, up, **f32)
+    dscores = (probs * (dprobs - jnp.sum(probs * dprobs, -1, keepdims=True)) * scaling).astype(jnp.bfloat16)
+    dqueries = jnp.einsum("hqk,khd->qhd", dscores, keys, **f32)
+    dkeys = jnp.einsum("hqk,qhd->khd", dscores, queries, **f32)
+    stacked = jnp.stack([dqueries, dkeys, dvalues], 1).reshape(length, 3, share).astype(jnp.bfloat16)
+    grads = lax.all_gather(stacked, ("gz", "gy"), axis=0).reshape(packs, parts, length, 3, share)
+    grads = grads.transpose(0, 2, 3, 1, 4).reshape(packs, length, 3, columns)
+    dnormed = jnp.einsum("prkc,kdc->prd", grads, weights, **f32).astype(jnp.bfloat16)
+    dnormed = lax.psum_scatter(dnormed, "gx", scatter_dimension=1, tiled=True)
+    dnormed = lax.all_to_all(dnormed.reshape(packs * rows, 1, block), "gz", 0, 1, tiled=True)
+    dxhat = dnormed.reshape(rows, width).astype(jnp.float32) * gain
+    total, weighted = lax.psum((jnp.sum(dxhat, -1), jnp.sum(dxhat * xhat, -1)), "gy")
+    gradient = inverse * (dxhat - total[:, None] / MODEL_WIDTH - xhat * (weighted[:, None] / MODEL_WIDTH))
+    return (attended, gradient)
+
+
 def solution(mesh):
+    def body(*arrays):
+        weights = arrays[4]
+        split = weights.shape[2] // HEAD_DIM
+        fits = split % mesh.shape["gy"] == 0 and weights.shape[1] % HEAD_DIM == 0
+        return (stationary if fits else on_device)(*arrays)
+
     return jax.shard_map(
-        on_device,
+        body,
         mesh=mesh,
         in_specs=(
             P(("gz", "gx"), "gy"),

time: 363 us -> 234 us (0.64)
  waiting for transfers between devices: 302 us -> 73.1 us
  local copies, waits for them, and re-layouts: 5.68 us -> 62.6 us
  blocking collectives: 17.2 us -> 37.7 us
  other arithmetic: 3.65 us -> 16.7 us
  starting transfers between devices: 0.16 us -> 8.85 us
    all_gather x1, waiting for transfers between devices: 233 us -> 33.2 us  [stationary(): lax.all_gather(stacked, ('gz', 'gy'), axis=0)]
    psum x2 -> x0, waiting for transfers between devices: 37 us -> none  [split_sum(): return lax.psum(partial_value, 'gy').astype(jnp.float32)]
    reshape x2 -> x9, local copies, waits for them, and re-layouts: 0.82 us -> 36.7 us  [the longest x2 14.5 us: stationary(): partial_value.astype(jnp.bfloat16).reshape(packs, length, 3, parts, share)]
    unnamed x4, waiting for transfers between devices: 0.73 us -> 22.5 us
    all_to_all x0 -> x2, blocking collectives: none -> 19.7 us  [the longest x1 11.6 us: stationary(): lax.all_to_all(normed.reshape(rows, packs, block), 'gz', 1, 0, tiled=True)]
    reduce_scatter x1, waiting for transfers between devices: 31 us -> 15.5 us  [stationary(): dnormed = lax.psum_scatter(dnormed, 'gx', scatter_dimension=1, tiled=True)]
    unnamed x12 -> x27, local copies, waits for them, and re-layouts: 0.17 us -> 12 us
    all_to_all x0 -> x2, starting transfers between devices: none -> 8.55 us  [the longest x1 4.32 us: stationary(): lax.all_to_all(dnormed.reshape(packs * rows, 1, block), 'gz', 0, 1, tiled...]
  transfers between devices with their start and end apart: 4 -> 5, of which waited for: 4 -> 4; matrix products, arithmetic and copies ran while one was open for 0% -> 7% of each run, Pallas kernels for 0% -> 0%
where the time goes in v1:
time: 234 us; the launch traced here: 232 us
  waiting for transfers between devices  73.1 us (31%)
  local copies, waits for them, and re-layouts  62.6 us (27%)
  blocking collectives  37.7 us (16%)
  matrix products  19.1 us (8%)
  other arithmetic  16.7 us (7%)
  between operations  13.9 us (6%)
  starting transfers between devices  8.85 us (4%)
    all_gather x1, waiting for transfers between devices, stationary(): lax.all_gather(stacked, ('gz', 'gy'), axis=0)  33.2 us
    unnamed x4, waiting for transfers between devices  22.5 us
    reduce_scatter x1, waiting for transfers between devices, stationary(): dnormed = lax.psum_scatter(dnormed, 'gx', scatter_dimension=1, tiled=True)  15.5 us
    reshape x2, local copies, waits for them, and re-layouts, stationary(): partial_value.astype(jnp.bfloat16).reshape(packs, length, 3, parts, share)  14.5 us
    unnamed x27, local copies, waits for them, and re-layouts  12 us
    all_to_all x1, blocking collectives, stationary(): lax.all_to_all(normed.reshape(rows, packs, block), 'gz', 1, 0, tiled=True)  11.6 us
    all_gather x1, blocking collectives, stationary(): moved = lax.all_gather(moved, 'gx', axis=1, tiled=True)  10.1 us
    all_to_all x1, blocking collectives, stationary(): lax.all_to_all(cotangent, 'gy', 1, 0, tiled=True)  8.1 us
  transfers between devices with their start and end apart: 5, of which 4 were waited for; matrix products, arithmetic and copies ran while one was open for 7% of the time, Pallas kernels for 0%

profile of v1, /device:TPU:1, one launch (start us, length us, event | category | flops | bytes accessed | tf_op | source)
XLA Modules:
  0.0 231.9 jit_solution(3211533130392646047)
XLA Ops:
  7.2 0.0 reduce-scatter.7.cloned.1.call-start
  7.2 0.8 iota_compare_fusion
  8.0 1.3 convert_reduce_fusion
  9.3 1.2 fusion.19
  10.5 1.8 all-gather.2
  12.4 1.1 select_reduce_fusion.1
  13.5 0.7 copy-done.1
  14.3 1.1 fusion.25
  15.3 11.6 %all_to_all.59 = bf16[32,4,768]{2,0,1:T(8,128)(2,1)S(1)} all-to-all(bf16[32,4,768]{2,0,1:T(8,128)(2,1)S(1)} %bitcast.109), channel_id=1, replica_groups=mesh['gx'=4,'gy'=2,'gz'=4] {'gz'}, dimensions={1} | all-to-all | bytes 393216 | tf_op jit(solution)/shard_map/all_to_all | solution.py:119
  27.0 10.1 %all-gather.1 = bf16[4,128,1,768]{3,1,0,2:T(8,128)(2,1)S(1)} all-gather(bf16[4,32,1,768]{3,1,0,2:T(8,128)(2,1)S(1)} %bitcast.111), channel_id=3, replica_groups=mesh['gx'=4,'gy'=2,'gz'=4] {'gx'}, dimensions={1}, use_global_device_ids=true | all-gather | bytes 983040 | tf_op jit(solution)/shard_map/all_gather | solution.py:121
  37.1 3.4 %fusion.5 = bf16[4,128,3,768]{3,1,2,0:T(8,128)(2,1)} fusion(bf16[3,768,768]{2,1,0:T(8,128)(2,1)S(1)} %copy-done, bf16[4,128,1,768]{3,1,0,2:T(8,128)(2,1)S(1)} %all-gather.1), kind=kOutput, calls=%fused_computation.6 | convolution fusion | flops 1813118976 | bytes 6684672 | tf_op jit(solution)/shard_map/prd,kdc->prkc/dot_general | solution.py:123
  40.5 5.8 %reshape.193 = bf16[4,128,3,2,384]{4,3,1,2,0:T(2,128)(2,1)} reshape(bf16[4,128,3,768]{3,1,2,0:T(8,128)(2,1)} %fusion.5) | data formatting | bytes 4718592 | tf_op jit(solution)/shard_map/reshape | solution.py:124
  46.3 8.8 %copy.79 = bf16[4,128,3,2,384]{1,3,0,4,2:T(2,128)(2,1)} copy(bf16[4,128,3,2,384]{4,3,1,2,0:T(2,128)(2,1)} %reshape.193) | data formatting | bytes 4718592 | tf_op jit(solution)/shard_map/reshape | solution.py:124
  55.1 6.4 %reshape.194 = bf16[1024,1152]{0,1:T(8,128)(2,1)} reshape(bf16[4,2,128,3,384]{2,1,0,4,3:T(2,128)(2,1)} %bitcast.102) | data formatting | bytes 4718592 | tf_op jit(solution)/shard_map/reshape | solution.py:125
  61.5 4.3 %copy.109 = bf16[1024,1152]{1,0:T(8,128)(2,1)} copy(bf16[1024,1152]{0,1:T(8,128)(2,1)} %reshape.194) | data formatting | bytes 4718592
  65.8 0.0 reduce-scatter.7.cloned.1.call-update
  65.8 0.0 all-gather.5.cloned.1.call-start
  65.9 0.9 copy.123
  66.8 8.1 %all_to_all.60 = bf16[64,2,384]{2,0,1:T(8,128)(2,1)} all-to-all(bf16[64,2,384]{2,0,1:T(8,128)(2,1)S(1)} %bitcast.118), channel_id=1, replica_groups=mesh['gx'=4,'gy'=2,'gz'=4] {'gy'}, dimensions={1} | all-to-all | bytes 196608 | tf_op jit(solution)/shard_map/all_to_all | solution.py:129
  74.9 1.6 reshape.196
  76.5 1.7 copy.93
  78.1 0.8 broadcast_compare_fusion
  79.0 22.4 %reduce-scatter.7.cloned.1.call-done = bf16[128,1152]{1,0:T(8,128)(2,1)} async-done(((bf16[1024,1152]{1,0:T(8,128)(2,1)}), bf16[128,1152]{1,0:T(8,128)(2,1)}) %reduce-scatter.7.cloned.1.call-update) | async-done | bytes 294928
  101.4 1.8 copy.110
  103.3 1.2 fusion.14
  104.4 0.7 copy-done.10
  105.1 0.7 fusion.35
  105.8 1.9 convolution_convert_fusion
  107.8 1.8 convolution_bitcast_fusion
  109.6 2.1 convolution_convert_fusion.1
  111.8 2.1 convolution_convert_fusion.2
  113.9 1.6 copy.96
  115.5 1.6 copy.95
  117.2 1.6 copy.94
  118.8 1.7 pad_maximum_fusion
  120.5 0.0 all-gather.5.cloned.1.call-update
  120.5 0.2 reduce-scatter.5.cloned.1.call-start
  120.8 33.2 %all-gather.5.cloned.1.call-done = bf16[8,128,3,384]{3,1,2,0:T(8,128)(2,1)} async-done(((bf16[1,128,3,384]{3,1,2,0:T(8,128)(2,1)}), bf16[8,128,3,384]{3,1,2,0:T(8,128)(2,1)}) %all-gather.5.cloned.1.call-update) | async-done | bytes 2359312 | tf_op jit(solution)/shard_map/all_gather | solution.py:146
  154.0 5.5 %copy.121 = bf16[4,2,128,3,384]{4,1,2,3,0:T(2,128)(2,1)} copy(bf16[4,2,128,3,384]{4,2,3,1,0:T(8,128)(2,1)} %bitcast.107) | data formatting | bytes 4718592 | tf_op jit(solution)/shard_map/reshape | solution.py:146
  159.5 6.4 %reshape.198 = bf16[4,128,3,768]{3,1,2,0:T(8,128)(2,1)} reshape(bf16[4,128,3,2,384]{4,3,1,2,0:T(2,128)(2,1)} %bitcast.103) | data formatting | bytes 4718592 | tf_op jit(solution)/shard_map/reshape | solution.py:147
  165.9 4.6 %bitcast_convert_fusion = bf16[4,128,768]{2,1,0:T(8,128)(2,1)} fusion(bf16[4,128,3,768]{3,1,2,0:T(8,128)(2,1)} %reshape.198, bf16[3,768,768]{2,1,0:T(8,128)(2,1)S(1)} %copy-done), kind=kOutput, calls=%fused_computation.7 | convolution fusion | flops 1812332544 | bytes 6684672 | tf_op jit(solution)/shard_map/prkc,kdc->prd/dot_general | solution.py:148
  170.5 0.0 reduce-scatter.5.cloned.1.call-update
  170.5 1.9 fusion.16
  172.4 1.7 copy.83
  174.1 1.6 all_to_all.47
  175.7 4.2 %all-to-all-start.1 = ((bf16[2,64,384]{2,1,0:T(8,128)(2,1)}), bf16[2,64,384]{2,1,0:T(8,128)(2,1)}, u32[]{:S(2)}, u32[]{:S(2)}) async-start(bf16[2,64,384]{2,1,0:T(8,128)(2,1)} %all_to_all.47), calls=%async_computation.1 | async-start | bytes 196608 | tf_op jit(solution)/shard_map/all_to_all | solution.py:139
  180.0 15.5 %reduce-scatter.5.cloned.1.call-done = bf16[4,32,768]{2,1,0:T(8,128)(2,1)} async-done(((bf16[4,128,768]{2,1,0:T(8,128)(2,1)}), bf16[4,32,768]{2,1,0:T(8,128)(2,1)}) %reduce-scatter.5.cloned.1.call-update) | async-done | bytes 196624 | tf_op jit(solution)/shard_map/reduce_scatter | solution.py:149
  195.5 0.6 broadcast.104
  196.1 2.4 %reduce.3 = bf16[128,768]{1,0:T(8,128)(2,1)} reduce(bf16[128,1,768]{2,0,1:T(8,128)(2,1)} %bitcast.119, bf16[]{:T(256)} %broadcast.104), dimensions={1}, to_apply=%copy.98.reduce_sub_computation | reduce | bytes 393218 | tf_op jit(solution)/shard_map/reshape | solution.py:150
  198.5 1.7 reshape.213
  200.1 4.3 %all-to-all-start.3 = ((bf16[4,2,12288]{2,1,0:T(2,128)(2,1)}), bf16[4,2,12288]{2,1,0:T(2,128)(2,1)}, u32[]{:S(2)}, u32[]{:S(2)}) async-start(bf16[4,2,12288]{2,1,0:T(2,128)(2,1)} %reshape.213), calls=%async_computation.4 | async-start | bytes 393216 | tf_op jit(solution)/shard_map/all_to_all | solution.py:150
  204.4 1.9 reduce_sum.110
  206.4 1.5 copy.115
  207.9 1.8 all-to-all-done.3
  209.7 2.2 reshape.214
  212.0 1.5 bitcast_convert_fusion.1
  213.5 1.3 copy.99
  214.7 0.1 copy.116
  214.8 0.2 fusion.26
  215.1 0.4 copy-done.4
  215.5 1.0 fusion.29
  216.5 6.1 %all-reduce = (f32[32]{0:T(128)S(1)}, f32[32]{0:T(128)}) all-reduce(f32[32]{0:T(128)S(1)} %fusion.26, f32[32]{0:T(128)} %fusion.29), channel_id=1, replica_groups=mesh['gx'=4,'gy'=2,'gz'=4] {'gy'}, use_global_device_ids=true, to_apply=%region_14.15 | all-reduce | flops 64 | bytes 512 | tf_op jit(solution)/shard_map/psum | solution.py:152
  222.6 0.7 broadcast_multiply_fusion
  223.3 2.1 fusion.28
  (27 shorter events, 0.1 us)
Async XLA Ops:
  7.2 29.9 %copy-start = (bf16[3,768,768]{2,1,0:T(8,128)(2,1)S(1)}, bf16[3,768,768]{2,1,0:T(8,128)(2,1)}, u32[]{:S(2)}) copy-start(bf16[3,768,768]{2,1,0:T(8,128)(2,1)} %param.11) | copy-start | bytes 10616836
  7.2 94.2 %reduce-scatter.7.cloned.1.call-start = ((), (), s32[]{:S(2)}) async-start(), calls=%async_computation.8 | async-start | bytes 2654208
  12.3 14.7 %copy-start.6 = (f32[32]{0:T(128)}, f32[32]{0:T(128)S(1)}, u32[]{:S(2)}) copy-start(f32[32]{0:T(128)S(1)} %broadcast_multiply_fusion.2) | copy-start | bytes 388
  12.3 14.6 %copy-start.8 = (f32[32]{0:T(128)}, f32[32]{0:T(128)S(1)}, u32[]{:S(2)}) copy-start(f32[32]{0:T(128)S(1)} %add_rsqrt_fusion) | copy-start | bytes 388
  13.5 0.8 copy-start.1
  65.8 88.2 %all-gather.5.cloned.1.call-start = ((), (), s32[]{:S(2)}) async-start(), calls=%async_computation.6 | async-start | bytes 2654208 | tf_op jit(solution)/shard_map/all_gather | solution.py:146
  104.4 0.7 copy-start.10
  120.5 75.0 %reduce-scatter.5.cloned.1.call-start = ((), (), s32[]{:S(2)}) async-start(), calls=%async_computation.7 | async-start | bytes 983040 | tf_op jit(solution)/shard_map/reduce_scatter | solution.py:149
  175.7 24.4 %all-to-all-start.1 = ((bf16[2,64,384]{2,1,0:T(8,128)(2,1)}), bf16[2,64,384]{2,1,0:T(8,128)(2,1)}, u32[]{:S(2)}, u32[]{:S(2)}) async-start(bf16[2,64,384]{2,1,0:T(8,128)(2,1)} %all_to_all.47), calls=%async_computation.1 | async-start | bytes 196608 | tf_op jit(solution)/shard_map/all_to_all | solution.py:139
  198.5 16.3 %copy-start.7 = (f32[32]{0:T(128)S(1)}, f32[32]{0:T(128)}, u32[]{:S(2)}) copy-start(f32[32]{0:T(128)} %copy-done.6) | copy-start | bytes 388
  198.5 16.3 %copy-start.9 = (f32[32]{0:T(128)S(1)}, f32[32]{0:T(128)}, u32[]{:S(2)}) copy-start(f32[32]{0:T(128)} %copy-done.8) | copy-start | bytes 388
  200.1 9.6 %all-to-all-start.3 = ((bf16[4,2,12288]{2,1,0:T(2,128)(2,1)}), bf16[4,2,12288]{2,1,0:T(2,128)(2,1)}, u32[]{:S(2)}, u32[]{:S(2)}) async-start(bf16[4,2,12288]{2,1,0:T(2,128)(2,1)} %reshape.213), calls=%async_computation.4 | async-start | bytes 393216 | tf_op jit(solution)/shard_map/all_to_all | solution.py:150
  212.0 2.9 %copy-start.2 = (f32[32,3072]{1,0:T(8,128)S(1)}, f32[32,3072]{1,0:T(8,128)}, u32[]{:S(2)}) copy-start(f32[32,3072]{1,0:T(8,128)} %copy-done.1) | copy-start | bytes 1179652
  212.0 2.9 %copy-start.3 = (bf16[32,3072]{1,0:T(8,128)(2,1)S(1)}, bf16[32,3072]{1,0:T(8,128)(2,1)}, u32[]{:S(2)}) copy-start(bf16[32,3072]{1,0:T(8,128)(2,1)} %param.7) | copy-start | bytes 589828
  212.0 3.6 %copy-start.5 = (f32[32,4,1,768]{3,1,0,2:T(4,128)S(1)}, f32[32,4,1,768]{3,1,0,2:T(4,128)}, u32[]{:S(2)}) copy-start(f32[32,4,1,768]{3,1,0,2:T(4,128)} %reduce_sum.110) | copy-start | bytes 1179652
  214.8 0.7 copy-start.4
Sparse Core Ops, SparseCore 0:
  66.0 35.3 reduce-scatter.6
  120.7 33.2 all-gather.4
  170.7 24.7 reduce-scatter.4

commit v2 on v0

--- a/solution.py
+++ b/solution.py
@@ -1,6 +1,10 @@
+import functools
+
 import jax
 import jax.numpy as jnp
 from jax import lax
+from jax.experimental import pallas as pl
+from jax.experimental.pallas import tpu as pltpu
 from jax.sharding import PartitionSpec as P
 
 MODEL_WIDTH = 6144
@@ -97,9 +101,305 @@
     return (attended, patch_gradient)
 
 
+MESH = pl.DeviceIdType.MESH
+F32 = dict(preferred_element_type=jnp.float32)
+
+
+def dot(a, b, da, db):
+    return lax.dot_general(a, b, (((da,), (db,)), ((), ())), **F32)
+
+
+def layer(
+    nx, nz, patches, modality, gains, biases, weights, segments, cotangent, attended, gradient,
+    held, mixed, xhat, gain, stat_out, stat_in, normed, rows_in, part_out, part_in, grads,
+    up, att_out, att_in, y_out, y_in, z_out, z_in,
+    local_sem, pair_send, pair_recv, a_send, a_recv, b_send, b_recv, c_send, c_recv,
+    p_send, p_recv, g_send, g_recv, h_send, h_recv, y_send, y_recv, z_send, z_recv,
+):
+    x, y, z = lax.axis_index("gx"), lax.axis_index("gy"), lax.axis_index("gz")
+    other = 1 - y
+    rows, width = patches.shape
+    block, columns = weights.shape[1:]
+    share = columns // 2
+    length = rows * nx
+    half = length // 2
+    count = 2 * width
+    order = (0,) + tuple(sorted(range(1, nz), key=lambda d: min(d, nz - d)))
+    sends = []
+
+    def send(source, target, send_sem, recv_sem, where):
+        copy = pltpu.make_async_remote_copy(
+            src_ref=source, dst_ref=target, send_sem=send_sem, recv_sem=recv_sem,
+            device_id=where, device_id_type=MESH,
+        )
+        copy.start()
+        sends.append(copy)
+        return copy
+
+    def along(axis, me, size, step):
+        return {axis: lax.rem(me + step + size, size)}
+
+    barrier = pltpu.get_barrier_semaphore()
+    pl.semaphore_signal(barrier, inc=1, device_id={"gy": other}, device_id_type=MESH)
+    for step in range(1, nx):
+        pl.semaphore_signal(barrier, inc=1, device_id=along("gx", x, nx, step), device_id_type=MESH)
+    for step in range(1, nz):
+        pl.semaphore_signal(barrier, inc=1, device_id=along("gz", z, nz, step), device_id_type=MESH)
+    own_columns = pl.ds(pl.multiple_of(y * share, HEAD_DIM), share)
+    other_columns = pl.ds(pl.multiple_of(other * share, HEAD_DIM), share)
+    keep = pltpu.make_async_copy(weights.at[:, :, own_columns], mixed.at[y], local_sem.at[0])
+    keep.start()
+    load = pltpu.make_async_copy(weights, held, local_sem.at[1])
+    load.start()
+
+    values = patches[...].astype(jnp.float32)
+    mine = jnp.sum(values, -1, keepdims=True) / width
+    spread = jnp.sum((values - mine) ** 2, -1, keepdims=True)
+    lane = lax.broadcasted_iota(jnp.int32, (rows, HEAD_DIM), 1)
+    stat_out[0] = jnp.where(lane == 0, mine, spread)
+    pl.semaphore_wait(barrier, nx + nz - 1)
+    to_pair = {"gy": other}
+    first = send(stat_out.at[0], stat_in.at[0], pair_send.at[0], pair_recv.at[0], to_pair)
+    swap_w = send(weights.at[:, :, other_columns], mixed.at[y], pair_send.at[1], pair_recv.at[1], to_pair)
+    swap_u = send(cotangent.at[:, other_columns], up.at[y], pair_send.at[2], pair_recv.at[2], to_pair)
+    up[y] = cotangent[:, own_columns]
+
+    diagonal = lax.broadcasted_iota(jnp.int32, (rows, rows), 0) == lax.broadcasted_iota(jnp.int32, (rows, rows), 1)
+    level = jnp.sum(jnp.where(diagonal, modality[...], 0), 1, keepdims=True)
+    for part in range(nz):
+        cols = slice(part * block, (part + 1) * block)
+        chosen = jnp.zeros((rows, block), jnp.float32)
+        for index in range(gains.shape[0]):
+            chosen = jnp.where(level == index, gains[index:index + 1, cols], chosen)
+        gain[:, cols] = chosen
+    first.wait_recv()
+    theirs = stat_in[0]
+    their_mean, their_spread = theirs[:, 0:1], theirs[:, 1:2]
+    average = (mine + their_mean) * 0.5
+    variance = (spread + their_spread + (mine - their_mean) ** 2 * (width * 0.5)) / count
+    inverse = lax.rsqrt(variance + EPS)
+    for part in range(nz):
+        cols = slice(part * block, (part + 1) * block)
+        offset = jnp.zeros((rows, block), jnp.float32)
+        for index in range(biases.shape[0]):
+            offset = jnp.where(level == index, biases[index:index + 1, cols], offset)
+        standard = (patches[:, cols].astype(jnp.float32) - average) * inverse
+        xhat[:, cols] = standard
+        normed[part] = (standard * gain[:, cols] + offset).astype(jnp.bfloat16)
+
+    place = pltpu.make_async_copy(normed.at[z], rows_in.at[y, 0, x], local_sem.at[2])
+    place.start()
+    arrive_a, arrive_b, arrive_c = {}, {}, {}
+    for e in range(1, nx):
+        arrive_b[0, e] = send(normed.at[z], rows_in.at[y, 0, x], b_send.at[0, e], b_recv.at[0, e], along("gx", x, nx, e))
+    for d in order[1:]:
+        arrive_a[d] = send(
+            normed.at[lax.rem(z + d, nz)], rows_in.at[y, d, x], a_send.at[d], a_recv.at[d], along("gz", z, nz, d)
+        )
+    for d in order[1:]:
+        arrive_a[d].wait_recv()
+        for e in range(1, nx):
+            arrive_b[d, e] = send(
+                rows_in.at[y, d, x], rows_in.at[y, d, x], b_send.at[d, e], b_recv.at[d, e], along("gx", x, nx, e)
+            )
+    place.wait()
+    keep.wait()
+    arrive_p = {}
+
+    def project(d):
+        arrive_c[d].wait_recv()
+        for k in range(3):
+            total = jnp.zeros((length, share), jnp.float32)
+            for g in range(2):
+                total = total + dot(rows_in[g, d].reshape(length, block), mixed[g, k], 1, 0)
+            part_out[d, :, k * share:(k + 1) * share] = total.astype(jnp.bfloat16)
+        if d:
+            arrive_p[d] = send(part_out.at[d], part_in.at[d], p_send.at[d], p_recv.at[d], along("gz", z, nz, -d))
+
+    last = None
+    for d in order:
+        for e in range(1, nx):
+            arrive_b[d, e].wait_recv()
+        arrive_c[d] = send(rows_in.at[y, d], rows_in.at[y, d], c_send.at[d], c_recv.at[d], to_pair)
+        if last is None:
+            swap_w.wait_recv()
+        else:
+            project(last)
+        last = d
+    project(last)
+
+    marks = segments[...]
+    diagonal = lax.broadcasted_iota(jnp.int32, (length, length), 0) == lax.broadcasted_iota(
+        jnp.int32, (length, length), 1
+    )
+    allowed = jnp.sum(jnp.where(diagonal, marks, 0), 1, keepdims=True) == marks
+    scaling = HEAD_DIM ** (-0.5)
+    load.wait()
+    swap_u.wait_recv()
+    for d in order[1:]:
+        arrive_p[d].wait_recv()
+    for h in range(share // HEAD_DIM):
+        taken = []
+        for k in range(3):
+            cols = slice(k * share + h * HEAD_DIM, k * share + (h + 1) * HEAD_DIM)
+            total = part_out[0, :, cols].astype(jnp.float32)
+            for d in order[1:]:
+                total = total + part_in[d, :, cols].astype(jnp.float32)
+            taken.append(total.astype(jnp.bfloat16))
+        query, key, value = taken
+        here = slice(h * HEAD_DIM, (h + 1) * HEAD_DIM)
+        above = up[:, :, here].reshape(length, HEAD_DIM)
+        exponent = jnp.where(allowed, jnp.exp(dot(query, key, 1, 1) * scaling), 0.0)
+        probs = exponent / jnp.sum(exponent, -1, keepdims=True)
+        probs_b = probs.astype(jnp.bfloat16)
+        att = dot(probs_b, value, 1, 0).astype(jnp.bfloat16)
+        att_out[:, :, here] = att.reshape(2, half, HEAD_DIM)
+        dprobs = dot(above, value, 1, 1)
+        dscores = probs * (dprobs - jnp.sum(probs * dprobs, -1, keepdims=True)) * scaling
+        dscores_b = dscores.astype(jnp.bfloat16)
+        found = (
+            dot(dscores_b, key, 1, 0),
+            dot(dscores_b, query, 0, 0),
+            dot(probs_b, above, 0, 0),
+        )
+        for k in range(3):
+            cols = slice(k * share + h * HEAD_DIM, k * share + (h + 1) * HEAD_DIM)
+            grads[0, y, :, cols] = found[k].astype(jnp.bfloat16)
+
+    arrive_g, arrive_h, arrive_y, arrive_z = {}, {}, {}, {}
+    for d in order[1:]:
+        arrive_g[d] = send(grads.at[0, y], grads.at[d, y], g_send.at[d], g_recv.at[d], along("gz", z, nz, d))
+    arrive_h[0] = send(grads.at[0, y], grads.at[0, y], h_send.at[0], h_recv.at[0], to_pair)
+    swap_a = send(att_out.at[other], att_in, pair_send.at[3], pair_recv.at[3], to_pair)
+
+    def back(d):
+        arrive_h[d].wait_recv()
+        total = jnp.zeros((length, block), jnp.float32)
+        for k in range(3):
+            for g in range(2):
+                total = total + dot(
+                    grads[d, g, :, k * share:(k + 1) * share], held[k, :, g * share:(g + 1) * share], 1, 1
+                )
+        y_out[d] = total.astype(jnp.bfloat16).reshape(nx, rows, block)
+        for e in range(1, nx):
+            arrive_y[d, e] = send(
+                y_out.at[d, lax.rem(x + e, nx)], y_in.at[d, e], y_send.at[d, e], y_recv.at[d, e], along("gx", x, nx, e)
+            )
+
+    def collect(d):
+        total = y_out[d, x].astype(jnp.float32)
+        for e in range(1, nx):
+            arrive_y[d, e].wait_recv()
+            total = total + y_in[d, e].astype(jnp.float32)
+        if d:
+            z_out[d] = total.astype(jnp.bfloat16)
+            arrive_z[d] = send(z_out.at[d], z_in.at[d], z_send.at[d], z_recv.at[d], along("gz", z, nz, -d))
+        else:
+            z_out[0] = total.astype(jnp.bfloat16)
+
+    back(0)
+    attended[:, own_columns] = att_out[y]
+    swap_a.wait_recv()
+    attended[:, other_columns] = att_in[...]
+    last = 0
+    for d in order[1:]:
+        arrive_g[d].wait_recv()
+        arrive_h[d] = send(grads.at[d, y], grads.at[d, y], h_send.at[d], h_recv.at[d], to_pair)
+        collect(last)
+        back(d)
+        last = d
+    collect(last)
+
+    plain = jnp.zeros((rows, 1), jnp.float32)
+    weighted = jnp.zeros((rows, 1), jnp.float32)
+    for d in order:
+        if d:
+            arrive_z[d].wait_recv()
+        cols = pl.ds(pl.multiple_of(lax.rem(z + d, nz) * block, HEAD_DIM), block)
+        dxhat = (z_in[d] if d else z_out[0]).astype(jnp.float32) * gain[:, cols]
+        gain[:, cols] = dxhat
+        plain = plain + jnp.sum(dxhat, -1, keepdims=True)
+        weighted = weighted + jnp.sum(dxhat * xhat[:, cols], -1, keepdims=True)
+    stat_out[1] = jnp.where(lane == 0, plain, weighted)
+    second = send(stat_out.at[1], stat_in.at[1], pair_send.at[4], pair_recv.at[4], to_pair)
+    second.wait_recv()
+    theirs = stat_in[1]
+    plain = (plain + theirs[:, 0:1]) / count
+    weighted = (weighted + theirs[:, 1:2]) / count
+    for part in range(nz):
+        cols = slice(part * block, (part + 1) * block)
+        gradient[:, cols] = inverse * (gain[:, cols] - plain - xhat[:, cols] * weighted)
+    for copy in sends:
+        copy.wait_send()
+
+
+def in_one_kernel(nx, nz, patches, modality, gains, biases, weights, segments, cotangent):
+    rows, width = patches.shape
+    block, columns = weights.shape[1:]
+    share, length = columns // 2, rows * nx
+    half = length // 2
+    bf16, f32 = jnp.bfloat16, jnp.float32
+    dma = pltpu.SemaphoreType.DMA
+    vmem = pl.BlockSpec(memory_space=pltpu.VMEM)
+    in_specs = [vmem] * 7
+    in_specs[4] = pl.BlockSpec(memory_space=pl.ANY)
+    return pl.pallas_call(
+        functools.partial(layer, nx, nz),
+        out_shape=(
+            jax.ShapeDtypeStruct((half, columns), bf16),
+            jax.ShapeDtypeStruct((rows, width), f32),
+        ),
+        in_specs=in_specs,
+        out_specs=(vmem, vmem),
+        scratch_shapes=[
+            pltpu.VMEM((3, block, columns), bf16),
+            pltpu.VMEM((2, 3, block, share), bf16),
+            pltpu.VMEM((rows, width), f32),
+            pltpu.VMEM((rows, width), f32),
+            pltpu.VMEM((2, rows, HEAD_DIM), f32),
+            pltpu.VMEM((2, rows, HEAD_DIM), f32),
+            pltpu.VMEM((nz, rows, block), bf16),
+            pltpu.VMEM((2, nz, nx, rows, block), bf16),
+            pltpu.VMEM((nz, length, 3 * share), bf16),
+            pltpu.VMEM((nz, length, 3 * share), bf16),
+            pltpu.VMEM((nz, 2, length, 3 * share), bf16),
+            pltpu.VMEM((2, half, share), bf16),
+            pltpu.VMEM((2, half, share), bf16),
+            pltpu.VMEM((half, share), bf16),
+            pltpu.VMEM((nz, nx, rows, block), bf16),
+            pltpu.VMEM((nz, nx, rows, block), bf16),
+            pltpu.VMEM((nz, rows, block), bf16),
+            pltpu.VMEM((nz, rows, block), bf16),
+            dma((3,)), dma((5,)), dma((5,)), dma((nz,)), dma((nz,)), dma((nz, nx)), dma((nz, nx)),
+            dma((nz,)), dma((nz,)), dma((nz,)), dma((nz,)), dma((nz,)), dma((nz,)), dma((nz,)), dma((nz,)),
+            dma((nz, nx)), dma((nz, nx)), dma((nz,)), dma((nz,)),
+        ],
+        compiler_params=pltpu.CompilerParams(
+            collective_id=0, has_side_effects=True, vmem_limit_bytes=56 << 20
+        ),
+    )(patches, modality.reshape(1, rows), gains, biases, weights, segments, cotangent)
+
+
 def solution(mesh):
+    nx, ny, nz = mesh.shape["gx"], mesh.shape["gy"], mesh.shape["gz"]
+
+    def body(*arrays):
+        patches, weights, segments = arrays[0], arrays[4], arrays[5]
+        block, columns = weights.shape[1:]
+        fits = (
+            ny == 2
+            and nx > 1
+            and nz > 1
+            and columns % (2 * HEAD_DIM) == 0
+            and block % HEAD_DIM == 0
+            and patches.shape[0] % 16 == 0
+            and segments.shape == (1, patches.shape[0] * nx)
+            and 2 * patches.shape[1] == MODEL_WIDTH
+        )
+        return in_one_kernel(nx, nz, *arrays) if fits else on_device(*arrays)
+
     return jax.shard_map(
-        on_device,
+        body,
         mesh=mesh,
         in_specs=(
             P(("gz", "gx"), "gy"),

time: 363 us -> 90.3 us (0.25)
  the two profiles are of different devices: /device:TPU:1 before, /device:TPU:9 now
where the time goes in v2:
time: 90.3 us; the launch traced here: 90.1 us
  Pallas kernels  86.2 us (95%)
  local copies, waits for them, and re-layouts  3.31 us (4%)
    pallas_call x1, Pallas kernels, in_one_kernel(): pl.pallas_call(functools.partial(layer, nx, nz), out_shape=(jax.ShapeDtyp...  86.2 us
    unnamed x2, local copies, waits for them, and re-layouts  3.31 us

profile of v2, /device:TPU:9, one launch (start us, length us, event | category | flops | bytes accessed | tf_op | source)
XLA Modules:
  0.0 90.1 jit_solution(3439029483531910876)
XLA Ops:
  0.6 86.2 %shard_map.86 = (bf16[64,768]{1,0:T(8,128)(2,1)}, f32[32,3072]{1,0:T(8,128)}) custom-call(bf16[32,3072]{1,0:T(8,128)(2,1)} %patches.1, s32[1,32]{1,0:T(1,128)} %bitcast.1, f32[3,3072]{1,0:T(4,128)} %gains.1, f32[3,3072]{1,0:T(4,128)} %biases.1, bf16[3,768,768]{2,1,0:T(8,128)(2,1)} %weights.1, s32[1,128]{1,0:T(1,128)} %segments.1, bf16[64,768]{1,0:T(8,128)(2,1)} %cotangent.1), custom_call_target="tpu_custom_call" | custom-call | tf_op jit(solution)/shard_map/pallas_call | solution.py:346
  86.8 1.5 %copy.11 = bf16[64,768]{1,0:T(8,128)(2,1)} copy(bf16[64,768]{1,0:T(8,128)(2,1)} %get-tuple-element.4) | data formatting | bytes 196608
  88.3 1.8 %copy.12 = f32[32,3072]{1,0:T(8,128)} copy(f32[32,3072]{1,0:T(8,128)} %get-tuple-element.5) | data formatting | bytes 786432

commit v3 on v2

--- a/solution.py
+++ b/solution.py
@@ -124,17 +124,36 @@
     length = rows * nx
     half = length // 2
     count = 2 * width
-    order = (0,) + tuple(sorted(range(1, nz), key=lambda d: min(d, nz - d)))
+    upper = lax.div(2 * z, nz)
+    outward = 1 - 2 * upper
+    at_edge = jnp.logical_or(z == 0, z == nz - 1)
+    queue = [upper * i + (1 - upper) * (nz - 1 - i) for i in range(nz)]
     sends = []
 
-    def send(source, target, send_sem, recv_sem, where):
+    def when(condition, action):
+        if condition is None:
+            action()
+        else:
+            pl.when(condition)(action)
+
+    def inside(index):
+        return jnp.logical_and(index >= 0, index < nz)
+
+    def send(source, target, send_sem, recv_sem, where, condition=None):
         copy = pltpu.make_async_remote_copy(
             src_ref=source, dst_ref=target, send_sem=send_sem, recv_sem=recv_sem,
             device_id=where, device_id_type=MESH,
         )
-        copy.start()
-        sends.append(copy)
+        when(condition, copy.start)
+        sends.append((condition, copy))
         return copy
+
+    def arrived(target, recv_sem, condition=None):
+        copy = pltpu.make_async_remote_copy(
+            src_ref=target, dst_ref=target, send_sem=local_sem.at[3], recv_sem=recv_sem,
+            device_id={"gy": other}, device_id_type=MESH,
+        )
+        when(condition, copy.wait_recv)
 
     def along(axis, me, size, step):
         return {axis: lax.rem(me + step + size, size)}
@@ -187,46 +206,62 @@
         xhat[:, cols] = standard
         normed[part] = (standard * gain[:, cols] + offset).astype(jnp.bfloat16)
 
-    place = pltpu.make_async_copy(normed.at[z], rows_in.at[y, 0, x], local_sem.at[2])
+    place = pltpu.make_async_copy(normed.at[z], rows_in.at[y, z, x], local_sem.at[2])
     place.start()
-    arrive_a, arrive_b, arrive_c = {}, {}, {}
+    for q in queue:
+        send(
+            normed.at[q], rows_in.at[y, z, x], a_send.at[q], a_recv.at[z], {"gz": q}, q != z
+        )
     for e in range(1, nx):
-        arrive_b[0, e] = send(normed.at[z], rows_in.at[y, 0, x], b_send.at[0, e], b_recv.at[0, e], along("gx", x, nx, e))
-    for d in order[1:]:
-        arrive_a[d] = send(
-            normed.at[lax.rem(z + d, nz)], rows_in.at[y, d, x], a_send.at[d], a_recv.at[d], along("gz", z, nz, d)
-        )
-    for d in order[1:]:
-        arrive_a[d].wait_recv()
+        send(normed.at[z], rows_in.at[y, z, x], b_send.at[z, e], b_recv.at[z, e], along("gx", x, nx, e))
+    for p in queue:
+        arrived(rows_in.at[y, p, x], a_recv.at[p], p != z)
         for e in range(1, nx):
-            arrive_b[d, e] = send(
-                rows_in.at[y, d, x], rows_in.at[y, d, x], b_send.at[d, e], b_recv.at[d, e], along("gx", x, nx, e)
+            send(
+                rows_in.at[y, p, x], rows_in.at[y, p, x], b_send.at[p, e], b_recv.at[p, e],
+                along("gx", x, nx, e), p != z,
             )
     place.wait()
     keep.wait()
-    arrive_p = {}
-
-    def project(d):
-        arrive_c[d].wait_recv()
+
+    def project(p):
+        arrived(rows_in.at[other, p], c_recv.at[p])
         for k in range(3):
             total = jnp.zeros((length, share), jnp.float32)
             for g in range(2):
-                total = total + dot(rows_in[g, d].reshape(length, block), mixed[g, k], 1, 0)
-            part_out[d, :, k * share:(k + 1) * share] = total.astype(jnp.bfloat16)
-        if d:
-            arrive_p[d] = send(part_out.at[d], part_in.at[d], p_send.at[d], p_recv.at[d], along("gz", z, nz, -d))
+                total = total + dot(rows_in[g, p].reshape(length, block), mixed[g, k], 1, 0)
+            part_out[p, :, k * share:(k + 1) * share] = total.astype(jnp.bfloat16)
+        send(
+            part_out.at[p], part_in.at[upper, p], p_send.at[p], p_recv.at[upper, p],
+            along("gz", z, nz, outward), jnp.logical_and(at_edge, p != z),
+        )
 
     last = None
-    for d in order:
+    for p in queue:
         for e in range(1, nx):
-            arrive_b[d, e].wait_recv()
-        arrive_c[d] = send(rows_in.at[y, d], rows_in.at[y, d], c_send.at[d], c_recv.at[d], to_pair)
+            arrived(rows_in.at[y, p, lax.rem(x - e + nx, nx)], b_recv.at[p, e])
+        send(rows_in.at[y, p], rows_in.at[y, p], c_send.at[p], c_recv.at[p], to_pair)
         if last is None:
             swap_w.wait_recv()
         else:
             project(last)
-        last = d
+        last = p
     project(last)
+
+    def add_in(side, p):
+        part_out[p] = (part_out[p].astype(jnp.float32) + part_in[side, p].astype(jnp.float32)).astype(jnp.bfloat16)
+
+    for t in range(nz - 1):
+        for way in (outward, -outward):
+            side = lax.div(1 - way, 2)
+            p = (1 - side) * (nz - 1 - t) + side * t
+            relays = jnp.logical_and((p - z) * way > 0, inside(z - way))
+            arrived(part_in.at[side, p], p_recv.at[side, p], relays)
+            when(relays, functools.partial(add_in, side, p))
+            send(
+                part_out.at[p], part_in.at[side, p], p_send.at[p], p_recv.at[side, p],
+                along("gz", z, nz, way), relays,
+            )
 
     marks = segments[...]
     diagonal = lax.broadcasted_iota(jnp.int32, (length, length), 0) == lax.broadcasted_iota(
@@ -236,16 +271,14 @@
     scaling = HEAD_DIM ** (-0.5)
     load.wait()
     swap_u.wait_recv()
-    for d in order[1:]:
-        arrive_p[d].wait_recv()
+    for side, present in ((0, z > 0), (1, z < nz - 1)):
+        arrived(part_in.at[side, z], p_recv.at[side, z], present)
+        when(present, functools.partial(add_in, side, z))
     for h in range(share // HEAD_DIM):
         taken = []
         for k in range(3):
             cols = slice(k * share + h * HEAD_DIM, k * share + (h + 1) * HEAD_DIM)
-            total = part_out[0, :, cols].astype(jnp.float32)
-            for d in order[1:]:
-                total = total + part_in[d, :, cols].astype(jnp.float32)
-            taken.append(total.astype(jnp.bfloat16))
+            taken.append(part_out[z, :, cols])
         query, key, value = taken
         here = slice(h * HEAD_DIM, (h + 1) * HEAD_DIM)
         above = up[:, :, here].reshape(length, HEAD_DIM)
@@ -264,59 +297,83 @@
         )
         for k in range(3):
             cols = slice(k * share + h * HEAD_DIM, k * share + (h + 1) * HEAD_DIM)
-            grads[0, y, :, cols] = found[k].astype(jnp.bfloat16)
-
-    arrive_g, arrive_h, arrive_y, arrive_z = {}, {}, {}, {}
-    for d in order[1:]:
-        arrive_g[d] = send(grads.at[0, y], grads.at[d, y], g_send.at[d], g_recv.at[d], along("gz", z, nz, d))
-    arrive_h[0] = send(grads.at[0, y], grads.at[0, y], h_send.at[0], h_recv.at[0], to_pair)
+            grads[z, y, :, cols] = found[k].astype(jnp.bfloat16)
+
+    def pass_on(p, way, condition):
+        send(
+            grads.at[p, y], grads.at[p, y], g_send.at[(1 - way) // 2, p], g_recv.at[p],
+            along("gz", z, nz, way), jnp.logical_and(condition, inside(z + way)),
+        )
+
+    for way in (1, -1):
+        pass_on(z, way, True)
+    send(grads.at[z, y], grads.at[z, y], h_send.at[z], h_recv.at[z], to_pair)
     swap_a = send(att_out.at[other], att_in, pair_send.at[3], pair_recv.at[3], to_pair)
 
-    def back(d):
-        arrive_h[d].wait_recv()
-        total = jnp.zeros((length, block), jnp.float32)
-        for k in range(3):
-            for g in range(2):
-                total = total + dot(
-                    grads[d, g, :, k * share:(k + 1) * share], held[k, :, g * share:(g + 1) * share], 1, 1
-                )
-        y_out[d] = total.astype(jnp.bfloat16).reshape(nx, rows, block)
+    def back(p, condition=None):
+        arrived(grads.at[p, other], h_recv.at[p], condition)
+
+        def multiply():
+            total = jnp.zeros((length, block), jnp.float32)
+            for k in range(3):
+                for g in range(2):
+                    total = total + dot(
+                        grads[p, g, :, k * share:(k + 1) * share], held[k, :, g * share:(g + 1) * share], 1, 1
+                    )
+            y_out[p] = total.astype(jnp.bfloat16).reshape(nx, rows, block)
+
+        when(condition, multiply)
         for e in range(1, nx):
-            arrive_y[d, e] = send(
-                y_out.at[d, lax.rem(x + e, nx)], y_in.at[d, e], y_send.at[d, e], y_recv.at[d, e], along("gx", x, nx, e)
+            send(
+                y_out.at[p, lax.rem(x + e, nx)], y_in.at[p, e], y_send.at[p, e], y_recv.at[p, e],
+                along("gx", x, nx, e), condition,
             )
 
-    def collect(d):
-        total = y_out[d, x].astype(jnp.float32)
+    def collect(p, condition=None):
         for e in range(1, nx):
-            arrive_y[d, e].wait_recv()
-            total = total + y_in[d, e].astype(jnp.float32)
-        if d:
-            z_out[d] = total.astype(jnp.bfloat16)
-            arrive_z[d] = send(z_out.at[d], z_in.at[d], z_send.at[d], z_recv.at[d], along("gz", z, nz, -d))
-        else:
-            z_out[0] = total.astype(jnp.bfloat16)
-
-    back(0)
+            arrived(y_in.at[p, e], y_recv.at[p, e], condition)
+
+        def add_up():
+            total = y_out[p, x].astype(jnp.float32)
+            for e in range(1, nx):
+                total = total + y_in[p, e].astype(jnp.float32)
+            if condition is None:
+                z_in[z] = total.astype(jnp.bfloat16)
+            else:
+                z_out[p] = total.astype(jnp.bfloat16)
+
+        when(condition, add_up)
+        if condition is not None:
+            send(z_out.at[p], z_in.at[z], z_send.at[p], z_recv.at[z], {"gz": p}, condition)
+
+    back(z)
     attended[:, own_columns] = att_out[y]
     swap_a.wait_recv()
     attended[:, other_columns] = att_in[...]
-    last = 0
-    for d in order[1:]:
-        arrive_g[d].wait_recv()
-        arrive_h[d] = send(grads.at[d, y], grads.at[d, y], h_send.at[d], h_recv.at[d], to_pair)
-        collect(last)
-        back(d)
-        last = d
-    collect(last)
+    waiting = [(z, None)]
+    for t in range(1, nz):
+        found = []
+        for way in (1, -1):
+            p = lax.rem(z - way * t + nz, nz)
+            present = inside(z - way * t)
+            arrived(grads.at[p, y], g_recv.at[p], present)
+            pass_on(p, way, present)
+            send(grads.at[p, y], grads.at[p, y], h_send.at[p], h_recv.at[p], to_pair, present)
+            found.append((p, present))
+        for p, present in waiting:
+            collect(p, present)
+        for p, present in found:
+            back(p, present)
+        waiting = found
+    for p, present in waiting:
+        collect(p, present)
 
     plain = jnp.zeros((rows, 1), jnp.float32)
     weighted = jnp.zeros((rows, 1), jnp.float32)
-    for d in order:
-        if d:
-            arrive_z[d].wait_recv()
-        cols = pl.ds(pl.multiple_of(lax.rem(z + d, nz) * block, HEAD_DIM), block)
-        dxhat = (z_in[d] if d else z_out[0]).astype(jnp.float32) * gain[:, cols]
+    for part in range(nz):
+        arrived(z_in.at[part], z_recv.at[part], z != part)
+        cols = slice(part * block, (part + 1) * block)
+        dxhat = z_in[part].astype(jnp.float32) * gain[:, cols]
         gain[:, cols] = dxhat
         plain = plain + jnp.sum(dxhat, -1, keepdims=True)
         weighted = weighted + jnp.sum(dxhat * xhat[:, cols], -1, keepdims=True)
@@ -329,8 +386,8 @@
     for part in range(nz):
         cols = slice(part * block, (part + 1) * block)
         gradient[:, cols] = inverse * (gain[:, cols] - plain - xhat[:, cols] * weighted)
-    for copy in sends:
-        copy.wait_send()
+    for condition, copy in sends:
+        when(condition, copy.wait_send)
 
 
 def in_one_kernel(nx, nz, patches, modality, gains, biases, weights, segments, cotangent):
@@ -361,7 +418,7 @@
             pltpu.VMEM((nz, rows, block), bf16),
             pltpu.VMEM((2, nz, nx, rows, block), bf16),
             pltpu.VMEM((nz, length, 3 * share), bf16),
-            pltpu.VMEM((nz, length, 3 * share), bf16),
+            pltpu.VMEM((2, nz, length, 3 * share), bf16),
             pltpu.VMEM((nz, 2, length, 3 * share), bf16),
             pltpu.VMEM((2, half, share), bf16),
             pltpu.VMEM((2, half, share), bf16),
@@ -370,8 +427,8 @@
             pltpu.VMEM((nz, nx, rows, block), bf16),
             pltpu.VMEM((nz, rows, block), bf16),
             pltpu.VMEM((nz, rows, block), bf16),
-            dma((3,)), dma((5,)), dma((5,)), dma((nz,)), dma((nz,)), dma((nz, nx)), dma((nz, nx)),
-            dma((nz,)), dma((nz,)), dma((nz,)), dma((nz,)), dma((nz,)), dma((nz,)), dma((nz,)), dma((nz,)),
+            dma((4,)), dma((5,)), dma((5,)), dma((nz,)), dma((nz,)), dma((nz, nx)), dma((nz, nx)),
+            dma((nz,)), dma((nz,)), dma((nz,)), dma((2, nz)), dma((2, nz)), dma((nz,)), dma((nz,)), dma((nz,)),
             dma((nz, nx)), dma((nz, nx)), dma((nz,)), dma((nz,)),
         ],
         compiler_params=pltpu.CompilerParams(

time: 90.3 us -> 80.3 us (0.89)
  the two profiles are of different devices: /device:TPU:9 before, /device:TPU:1 now
where the time goes in v3:
time: 80.3 us; the launch traced here: 80.1 us
  Pallas kernels  76.2 us (95%)
  local copies, waits for them, and re-layouts  3.31 us (4%)
    pallas_call x1, Pallas kernels, in_one_kernel(): pl.pallas_call(functools.partial(layer, nx, nz), out_shape=(jax.ShapeDtyp...  76.2 us
    unnamed x2, local copies, waits for them, and re-layouts  3.31 us

profile of v3, /device:TPU:1, one launch (start us, length us, event | category | flops | bytes accessed | tf_op | source)
XLA Modules:
  0.0 80.1 jit_solution(18069035023442537267)
XLA Ops:
  0.6 76.2 %shard_map.86 = (bf16[64,768]{1,0:T(8,128)(2,1)}, f32[32,3072]{1,0:T(8,128)}) custom-call(bf16[32,3072]{1,0:T(8,128)(2,1)} %patches.1, s32[1,32]{1,0:T(1,128)} %bitcast.1, f32[3,3072]{1,0:T(4,128)} %gains.1, f32[3,3072]{1,0:T(4,128)} %biases.1, bf16[3,768,768]{2,1,0:T(8,128)(2,1)} %weights.1, s32[1,128]{1,0:T(1,128)} %segments.1, bf16[64,768]{1,0:T(8,128)(2,1)} %cotangent.1), custom_call_target="tpu_custom_call" | custom-call | tf_op jit(solution)/shard_map/pallas_call | solution.py:403
  76.8 1.5 %copy.11 = bf16[64,768]{1,0:T(8,128)(2,1)} copy(bf16[64,768]{1,0:T(8,128)(2,1)} %get-tuple-element.4) | data formatting | bytes 196608
  78.4 1.8 %copy.12 = f32[32,3072]{1,0:T(8,128)} copy(f32[32,3072]{1,0:T(8,128)} %get-tuple-element.5) | data formatting | bytes 786432

commit v4 on v3

--- a/solution.py
+++ b/solution.py
@@ -128,6 +128,7 @@
     outward = 1 - 2 * upper
     at_edge = jnp.logical_or(z == 0, z == nz - 1)
     queue = [upper * i + (1 - upper) * (nz - 1 - i) for i in range(nz)]
+    cuts = [(c, pl.ds(c * half, half)) for c in range(2)]
     sends = []
 
     def when(condition, action):
@@ -231,10 +232,11 @@
             for g in range(2):
                 total = total + dot(rows_in[g, p].reshape(length, block), mixed[g, k], 1, 0)
             part_out[p, :, k * share:(k + 1) * share] = total.astype(jnp.bfloat16)
-        send(
-            part_out.at[p], part_in.at[upper, p], p_send.at[p], p_recv.at[upper, p],
-            along("gz", z, nz, outward), jnp.logical_and(at_edge, p != z),
-        )
+        for c, cut in cuts:
+            send(
+                part_out.at[p, cut], part_in.at[upper, p, cut], p_send.at[p, c], p_recv.at[upper, p, c],
+                along("gz", z, nz, outward), jnp.logical_and(at_edge, p != z),
+            )
 
     last = None
     for p in queue:
@@ -248,20 +250,22 @@
         last = p
     project(last)
 
-    def add_in(side, p):
-        part_out[p] = (part_out[p].astype(jnp.float32) + part_in[side, p].astype(jnp.float32)).astype(jnp.bfloat16)
+    def add_in(side, p, cut):
+        total = part_out[p, cut].astype(jnp.float32) + part_in[side, p, cut].astype(jnp.float32)
+        part_out[p, cut] = total.astype(jnp.bfloat16)
 
     for t in range(nz - 1):
         for way in (outward, -outward):
             side = lax.div(1 - way, 2)
             p = (1 - side) * (nz - 1 - t) + side * t
             relays = jnp.logical_and((p - z) * way > 0, inside(z - way))
-            arrived(part_in.at[side, p], p_recv.at[side, p], relays)
-            when(relays, functools.partial(add_in, side, p))
-            send(
-                part_out.at[p], part_in.at[side, p], p_send.at[p], p_recv.at[side, p],
-                along("gz", z, nz, way), relays,
-            )
+            for c, cut in cuts:
+                arrived(part_in.at[side, p, cut], p_recv.at[side, p, c], relays)
+                when(relays, functools.partial(add_in, side, p, cut))
+                send(
+                    part_out.at[p, cut], part_in.at[side, p, cut], p_send.at[p, c], p_recv.at[side, p, c],
+                    along("gz", z, nz, way), relays,
+                )
 
     marks = segments[...]
     diagonal = lax.broadcasted_iota(jnp.int32, (length, length), 0) == lax.broadcasted_iota(
@@ -272,8 +276,9 @@
     load.wait()
     swap_u.wait_recv()
     for side, present in ((0, z > 0), (1, z < nz - 1)):
-        arrived(part_in.at[side, z], p_recv.at[side, z], present)
-        when(present, functools.partial(add_in, side, z))
+        for c, cut in cuts:
+            arrived(part_in.at[side, z, cut], p_recv.at[side, z, c], present)
+            when(present, functools.partial(add_in, side, z, cut))
     for h in range(share // HEAD_DIM):
         taken = []
         for k in range(3):
@@ -299,19 +304,21 @@
             cols = slice(k * share + h * HEAD_DIM, k * share + (h + 1) * HEAD_DIM)
             grads[z, y, :, cols] = found[k].astype(jnp.bfloat16)
 
-    def pass_on(p, way, condition):
+    def pass_on(p, way, condition, c, cut):
         send(
-            grads.at[p, y], grads.at[p, y], g_send.at[(1 - way) // 2, p], g_recv.at[p],
+            grads.at[p, y, cut], grads.at[p, y, cut], g_send.at[(1 - way) // 2, p, c], g_recv.at[p, c],
             along("gz", z, nz, way), jnp.logical_and(condition, inside(z + way)),
         )
 
-    for way in (1, -1):
-        pass_on(z, way, True)
-    send(grads.at[z, y], grads.at[z, y], h_send.at[z], h_recv.at[z], to_pair)
+    for c, cut in cuts:
+        for way in (1, -1):
+            pass_on(z, way, True, c, cut)
+        send(grads.at[z, y, cut], grads.at[z, y, cut], h_send.at[z, c], h_recv.at[z, c], to_pair)
     swap_a = send(att_out.at[other], att_in, pair_send.at[3], pair_recv.at[3], to_pair)
 
     def back(p, condition=None):
-        arrived(grads.at[p, other], h_recv.at[p], condition)
+        for c, cut in cuts:
+            arrived(grads.at[p, other, cut], h_recv.at[p, c], condition)
 
         def multiply():
             total = jnp.zeros((length, block), jnp.float32)
@@ -353,13 +360,17 @@
     waiting = [(z, None)]
     for t in range(1, nz):
         found = []
-        for way in (1, -1):
-            p = lax.rem(z - way * t + nz, nz)
-            present = inside(z - way * t)
-            arrived(grads.at[p, y], g_recv.at[p], present)
-            pass_on(p, way, present)
-            send(grads.at[p, y], grads.at[p, y], h_send.at[p], h_recv.at[p], to_pair, present)
-            found.append((p, present))
+        for c, cut in cuts:
+            for way in (1, -1):
+                p = lax.rem(z - way * t + nz, nz)
+                present = inside(z - way * t)
+                arrived(grads.at[p, y, cut], g_recv.at[p, c], present)
+                pass_on(p, way, present, c, cut)
+                send(
+                    grads.at[p, y, cut], grads.at[p, y, cut], h_send.at[p, c], h_recv.at[p, c], to_pair, present
+                )
+                if c == 0:
+                    found.append((p, present))
         for p, present in waiting:
             collect(p, present)
         for p, present in found:
@@ -428,7 +439,8 @@
             pltpu.VMEM((nz, rows, block), bf16),
             pltpu.VMEM((nz, rows, block), bf16),
             dma((4,)), dma((5,)), dma((5,)), dma((nz,)), dma((nz,)), dma((nz, nx)), dma((nz, nx)),
-            dma((nz,)), dma((nz,)), dma((nz,)), dma((2, nz)), dma((2, nz)), dma((nz,)), dma((nz,)), dma((nz,)),
+            dma((nz,)), dma((nz,)), dma((nz, 2)), dma((2, nz, 2)), dma((2, nz, 2)), dma((nz, 2)),
+            dma((nz, 2)), dma((nz, 2)),
             dma((nz, nx)), dma((nz, nx)), dma((nz,)), dma((nz,)),
         ],
         compiler_params=pltpu.CompilerParams(
@@ -450,6 +462,7 @@
             and columns % (2 * HEAD_DIM) == 0
             and block % HEAD_DIM == 0
             and patches.shape[0] % 16 == 0
+            and patches.shape[0] * nx % 32 == 0
             and segments.shape == (1, patches.shape[0] * nx)
             and 2 * patches.shape[1] == MODEL_WIDTH
         )

time: 80.3 us -> 80.3 us (level)
  no operation moved by 1% of the time
where the time goes in v4:
time: 80.3 us; the launch traced here: 80.1 us
  Pallas kernels  76.1 us (95%)
  local copies, waits for them, and re-layouts  3.31 us (4%)
    pallas_call x1, Pallas kernels, in_one_kernel(): pl.pallas_call(functools.partial(layer, nx, nz), out_shape=(jax.ShapeDtyp...  76.1 us
    unnamed x2, local copies, waits for them, and re-layouts  3.31 us

profile of v4, /device:TPU:1, one launch (start us, length us, event | category | flops | bytes accessed | tf_op | source)
XLA Modules:
  0.0 80.1 jit_solution(2578788392522599428)
XLA Ops:
  0.6 76.1 %shard_map.86 = (bf16[64,768]{1,0:T(8,128)(2,1)}, f32[32,3072]{1,0:T(8,128)}) custom-call(bf16[32,3072]{1,0:T(8,128)(2,1)} %patches.1, s32[1,32]{1,0:T(1,128)} %bitcast.1, f32[3,3072]{1,0:T(4,128)} %gains.1, f32[3,3072]{1,0:T(4,128)} %biases.1, bf16[3,768,768]{2,1,0:T(8,128)(2,1)} %weights.1, s32[1,128]{1,0:T(1,128)} %segments.1, bf16[64,768]{1,0:T(8,128)(2,1)} %cotangent.1), custom_call_target="tpu_custom_call" | custom-call | tf_op jit(solution)/shard_map/pallas_call | solution.py:414
  76.8 1.5 %copy.11 = bf16[64,768]{1,0:T(8,128)(2,1)} copy(bf16[64,768]{1,0:T(8,128)(2,1)} %get-tuple-element.4) | data formatting | bytes 196608
  78.3 1.8 %copy.12 = f32[32,3072]{1,0:T(8,128)} copy(f32[32,3072]{1,0:T(8,128)} %get-tuple-element.5) | data formatting | bytes 786432

commit v5 on v4

--- a/solution.py
+++ b/solution.py
@@ -9,6 +9,7 @@
 
 MODEL_WIDTH = 6144
 HEAD_DIM = 128
+CUTS = 4
 
 
 EPS = 1e-06
@@ -128,7 +129,7 @@
     outward = 1 - 2 * upper
     at_edge = jnp.logical_or(z == 0, z == nz - 1)
     queue = [upper * i + (1 - upper) * (nz - 1 - i) for i in range(nz)]
-    cuts = [(c, pl.ds(c * half, half)) for c in range(2)]
+    cuts = [(c, pl.ds(c * (length // CUTS), length // CUTS)) for c in range(CUTS)]
     sends = []
 
     def when(condition, action):
@@ -439,8 +440,8 @@
             pltpu.VMEM((nz, rows, block), bf16),
             pltpu.VMEM((nz, rows, block), bf16),
             dma((4,)), dma((5,)), dma((5,)), dma((nz,)), dma((nz,)), dma((nz, nx)), dma((nz, nx)),
-            dma((nz,)), dma((nz,)), dma((nz, 2)), dma((2, nz, 2)), dma((2, nz, 2)), dma((nz, 2)),
-            dma((nz, 2)), dma((nz, 2)),
+            dma((nz,)), dma((nz,)), dma((nz, CUTS)), dma((2, nz, CUTS)), dma((2, nz, CUTS)), dma((nz, CUTS)),
+            dma((nz, CUTS)), dma((nz, CUTS)),
             dma((nz, nx)), dma((nz, nx)), dma((nz,)), dma((nz,)),
         ],
         compiler_params=pltpu.CompilerParams(
@@ -462,7 +463,7 @@
             and columns % (2 * HEAD_DIM) == 0
             and block % HEAD_DIM == 0
             and patches.shape[0] % 16 == 0
-            and patches.shape[0] * nx % 32 == 0
+            and patches.shape[0] * nx % (16 * CUTS) == 0
             and segments.shape == (1, patches.shape[0] * nx)
             and 2 * patches.shape[1] == MODEL_WIDTH
         )

time: 80.3 us -> 79.7 us (level)
  no operation moved by 1% of the time
where the time goes in v5:
time: 79.7 us; the launch traced here: 79.4 us
  Pallas kernels  75.5 us (95%)
  local copies, waits for them, and re-layouts  3.31 us (4%)
    pallas_call x1, Pallas kernels, in_one_kernel(): pl.pallas_call(functools.partial(layer, nx, nz), out_shape=(jax.ShapeDtyp...  75.5 us
    unnamed x2, local copies, waits for them, and re-layouts  3.31 us

profile of v5, /device:TPU:1, one launch (start us, length us, event | category | flops | bytes accessed | tf_op | source)
XLA Modules:
  0.0 79.4 jit_solution(4526082315534385699)
XLA Ops:
  0.6 75.5 %shard_map.86 = (bf16[64,768]{1,0:T(8,128)(2,1)}, f32[32,3072]{1,0:T(8,128)}) custom-call(bf16[32,3072]{1,0:T(8,128)(2,1)} %patches.1, s32[1,32]{1,0:T(1,128)} %bitcast.1, f32[3,3072]{1,0:T(4,128)} %gains.1, f32[3,3072]{1,0:T(4,128)} %biases.1, bf16[3,768,768]{2,1,0:T(8,128)(2,1)} %weights.1, s32[1,128]{1,0:T(1,128)} %segments.1, bf16[64,768]{1,0:T(8,128)(2,1)} %cotangent.1), custom_call_target="tpu_custom_call" | custom-call | tf_op jit(solution)/shard_map/pallas_call | solution.py:415
  76.1 1.5 %copy.11 = bf16[64,768]{1,0:T(8,128)(2,1)} copy(bf16[64,768]{1,0:T(8,128)(2,1)} %get-tuple-element.4) | data formatting | bytes 196608
  77.7 1.8 %copy.12 = f32[32,3072]{1,0:T(8,128)} copy(f32[32,3072]{1,0:T(8,128)} %get-tuple-element.5) | data formatting | bytes 786432
